TPU v7x, 32 devices: a whole 2x2x4 slice. The times are simulated.
32 devices in a mesh: grp: 2 (over y), img: 4 (over z), gz: 4 (over x, core).
Axes of the slice: x: 2, y: 2, z: 4, core: 2. Of those that a mesh axis runs over, the one named last changes fastest.
Arguments:
- ordering_variable: bfloat16 [16, 16, 64, 256], P(('grp', 'img'), 'gz'), parts along dimension 0, may hold values from 0 to 1
- lattice_shift_field: bfloat16 [3, 16, 16, 64, 256], P(None, ('grp', 'img'), 'gz'), parts along dimension 1, may hold values from -3 to 3
- eigenstrain_mismatch: float32 [2], P('grp'), parts along dimension 0, may hold values from 0.3 to 1
- thermal_state_kelvin: float32 [2], P('grp'), parts along dimension 0, may hold values from 1100 to 1300
Outputs:
- string: bfloat16 [16, 16, 64, 256], P(('grp', 'img'), 'gz'), parts along dimension 0
- moved: bfloat16 [3, 16, 16, 64, 256], P(None, ('grp', 'img'), 'gz'), parts along dimension 1
There are 2 independent parts, one for each index of `grp`. A program takes and returns all parts, laid end to end along the dimension named above; each array names one. Nothing has to cross between parts.
All inputs are finite; a program needn't handle non-finite values.
Results may differ from a plain program's by a relative error of at most 0.0046.
Values may be sent and summed in bfloat16 or wider, within the bound.
A program may use at most 64 MiB of HBM per device.

v0:
```python
import jax
import jax.numpy as jnp
from jax import lax
from jax.sharding import PartitionSpec as P

stiff_eleven = 2.5
stiff_twelve = 1.5
stiff_shear = 1.2
barrier = 1.0
latent_enthalpy = 8.0
dissolution_limit_kelvin = 1250.0
gradient_coef = 1.0
mobility = 0.1
elastic_step = 0.03
epsilon = 1e-06


def padded(cells, sides, width, closed):
    for axis, dim in sides:
        count = lax.axis_size(axis)
        ends = count if closed else count - 1
        head = lax.slice_in_dim(cells, 0, width, axis=dim)
        tail = lax.slice_in_dim(cells, cells.shape[dim] - width, cells.shape[dim], axis=dim)
        cells = jnp.concatenate(
            [
                lax.ppermute(tail, axis, [(i, (i + 1) % count) for i in range(ends)]),
                cells,
                lax.ppermute(head, axis, [((i + 1) % count, i) for i in range(ends)]),
            ],
            axis=dim,
        )
    return cells


def switching(value):
    return value * value * (3.0 - 2.0 * value)


def switching_slope(value):
    return 6.0 * value * (1.0 - value)


def well_slope(value):
    return 2.0 * value * (1.0 - value) * (1.0 - 2.0 * value)


def cubic_stress(slopes, eigen):
    strain_xx = slopes[0] + eigen
    strain_yy = slopes[1] + eigen
    strain_zz = slopes[2] + eigen
    return (
        stiff_eleven * strain_xx + stiff_twelve * (strain_yy + strain_zz),
        stiff_eleven * strain_yy + stiff_twelve * (strain_xx + strain_zz),
        stiff_eleven * strain_zz + stiff_twelve * (strain_xx + strain_yy),
        stiff_shear * (slopes[3] + slopes[4]),
        stiff_shear * (slopes[5] + slopes[6]),
        stiff_shear * (slopes[7] + slopes[8]),
    )


def across_x(field):
    return jnp.roll(field, -1, 2) - field


def transverse_y_term(field):
    return jnp.roll(field, -1, 3) - field


def plane_stress(order_planes, shifts, homogeneous, misfit_value):
    eigen = homogeneous[:, None, None, None] - misfit_value * switching(order_planes)
    lower = shifts[:, :, :-1]
    rise = shifts[:, :, 1:] - lower
    slopes = (
        across_x(lower[0]),
        transverse_y_term(lower[1]),
        rise[2],
        across_x(lower[1]),
        transverse_y_term(lower[0]),
        across_x(lower[2]),
        rise[0],
        transverse_y_term(lower[2]),
        rise[1],
    )
    return cubic_stress(slopes, eigen)


def behind_x(field):
    return field - jnp.roll(field, 1, 2)


def behind_y(field):
    return field - jnp.roll(field, 1, 3)


def trailing_z_term(field, under):
    return field - jnp.concatenate([under, field[:, :-1]], axis=1)


def shards(ordering_variable, lattice_shift_field, eigenstrain_mismatch, thermal_state_kelvin):
    misfit_value = eigenstrain_mismatch[0]
    chemical_free_energy_gain = (
        latent_enthalpy
        * (thermal_state_kelvin[0] - dissolution_limit_kelvin)
        / dissolution_limit_kelvin
    )
    local_images = ordering_variable.shape[0]
    cells = (
        ordering_variable.shape[1]
        * lax.axis_size("gz")
        * ordering_variable.shape[2]
        * ordering_variable.shape[3]
    )
    order = ordering_variable.astype(jnp.float32)
    shifts = lattice_shift_field.astype(jnp.float32)
    partial_h = jnp.sum(switching(order), axis=(1, 2, 3))
    homogeneous = misfit_value * (lax.psum(partial_h, "gz") / cells)
    wide_order, wide_shift = (
        padded(ordering_variable[None], (("gz", 2),), 1, True),
        padded(lattice_shift_field, (("gz", 2),), 1, True),
    )
    wide_order = wide_order[0].astype(jnp.float32)
    stress_all = plane_stress(
        wide_order[:, :-1], wide_shift.astype(jnp.float32), homogeneous, misfit_value
    )
    stress = tuple((component[:, 1:] for component in stress_all))
    beneath = (stress_all[4][:, :1], stress_all[5][:, :1], stress_all[2][:, :1])
    order_below = wide_order[:, :1]
    order_above = wide_order[:, -1:]
    force = jnp.stack(
        [
            behind_x(stress[0]) + behind_y(stress[3]) + trailing_z_term(stress[4], beneath[0]),
            behind_x(stress[3]) + behind_y(stress[1]) + trailing_z_term(stress[5], beneath[1]),
            behind_x(stress[4]) + behind_y(stress[5]) + trailing_z_term(stress[2], beneath[2]),
        ]
    )
    moved = (shifts + elastic_step * force).astype(jnp.bfloat16)
    column = jnp.concatenate([order_below, order, order_above], axis=1)
    laplace = (
        column[:, :-2]
        + column[:, 2:]
        + (jnp.roll(order, 1, 2) + jnp.roll(order, -1, 2))
        + (jnp.roll(order, 1, 3) + jnp.roll(order, -1, 3))
        - 6.0 * order
    )
    potential = (
        barrier * well_slope(order)
        + chemical_free_energy_gain * switching_slope(order)
        - gradient_coef * laplace
        - misfit_value * switching_slope(order) * (stress[0] + stress[1] + stress[2])
    )
    relaxed = (order - mobility * potential).astype(jnp.bfloat16)
    widened = padded(relaxed, (("img", 0),), 1, False).astype(jnp.float32)
    current = widened[1:-1]
    following = widened[2:]
    previous = widened[:-2]
    local_squares = jnp.sum((following - current) ** 2, axis=(1, 2, 3))
    total_images = local_images * lax.axis_size("img")
    first = lax.axis_index("img") * local_images
    squares = lax.psum(local_squares, "gz")
    gaps = lax.all_gather(jnp.sqrt(squares / cells + epsilon), "img", axis=0, tiled=True)
    used = gaps[: total_images - 1]
    single = jnp.ones((1,), jnp.float32)
    arc = jnp.concatenate([jnp.zeros((1,), jnp.float32), jnp.cumsum(used)])
    below_gap = jnp.concatenate([single, used])
    above_gap = jnp.concatenate([used, single])
    positions = first + jnp.arange(local_images, dtype=jnp.int32)
    target = arc[-1] * (positions.astype(jnp.float32) / (total_images - 1))
    arc_here = lax.dynamic_slice_in_dim(arc, first, local_images)
    back = jnp.clip(
        (arc_here - target) / lax.dynamic_slice_in_dim(below_gap, first, local_images), 0.0, 1.0
    )
    ahead = jnp.clip(
        (target - arc_here) / lax.dynamic_slice_in_dim(above_gap, first, local_images), 0.0, 1.0
    )
    string = (
        current
        + ahead[:, None, None, None] * (following - current)
        + back[:, None, None, None] * (previous - current)
    ).astype(jnp.bfloat16)
    return (string, moved)


def solution(mesh):
    in_specs = (
        P(("grp", "img"), "gz", None, None),
        P(None, ("grp", "img"), "gz", None, None),
        P("grp"),
        P("grp"),
    )
    out_specs = (P(("grp", "img"), "gz", None, None), P(None, ("grp", "img"), "gz", None, None))
    return jax.shard_map(shards, mesh=mesh, in_specs=in_specs, out_specs=out_specs, check_vma=False)
```

profile of v0, /device:TPU:0, one launch (start us, length us, event | category | flops | bytes accessed | tf_op | source)
XLA Modules:
  0.0 57.5 jit_solution(13908369728419254603)
XLA Ops:
  0.6 1.1 %fusion.47 = (bf16[3,2,1,64,256]{4,3,2,1,0:T(8,128)(2,1)S(1)}, bf16[3,2,1,64,256]{4,3,2,1,0:T(8,128)(2,1)S(1)}) fusion(bf16[3,2,4,64,256]{4,3,2,1,0:T(8,128)(2,1)} %param.5), kind=kLoop, calls=%fused_computation.96 | loop fusion | bytes 786432 | tf_op jit(solution)/shard_map/slice | solution.py:23
  1.7 0.5 collective-permute-start.2
  2.3 2.0 %collective-permute-start.3 = (bf16[3,2,1,64,256]{4,3,2,1,0:T(8,128)(2,1)S(1)}, bf16[3,2,1,64,256]{4,3,2,1,0:T(8,128)(2,1)S(1)}, u32[]{:S(2)}, u32[]{:S(2)}) collective-permute-start(bf16[3,2,1,64,256]{4,3,2,1,0:T(8,128)(2,1)S(1)} %get-tuple-element.16), channel_id=1, source_target_pairs={{1,0},{2,1},{3,2},{0,3},{5,4},{6,5},{7,6},{4,7},{9,8},{10,9},{11,1... | collective-permute-start | bytes 589832 | tf_op jit(solution)/shard_map/ppermute | solution.py:28
  4.3 1.5 %fusion.50 = (bf16[1,2,1,64,256]{4,3,2,1,0:T(8,128)(2,1)}, bf16[1,2,1,64,256]{4,3,2,1,0:T(8,128)(2,1)}) fusion(bf16[1,2,4,64,256]{4,3,2,1,0:T(8,128)(2,1)} %bitcast.65), kind=kLoop, calls=%fused_computation.99 | loop fusion | bytes 262144 | tf_op jit(solution)/shard_map/slice | solution.py:23
  5.8 0.6 %collective-permute-start = (bf16[1,2,1,64,256]{4,3,2,1,0:T(8,128)(2,1)}, bf16[1,2,1,64,256]{4,3,2,1,0:T(8,128)(2,1)S(1)}, u32[]{:S(2)}, u32[]{:S(2)}) collective-permute-start(bf16[1,2,1,64,256]{4,3,2,1,0:T(8,128)(2,1)} %get-tuple-element.23), channel_id=1, source_target_pairs={{0,1},{1,2},{2,3},{3,0},{4,5},{5,6},{6,7},{7,4},{8,9},{9,10},{10,1... | collective-permute-start | bytes 196616 | tf_op jit(solution)/shard_map/ppermute | solution.py:26
  6.4 1.1 %collective-permute-start.1 = (bf16[1,2,1,64,256]{4,3,2,1,0:T(8,128)(2,1)}, bf16[1,2,1,64,256]{4,3,2,1,0:T(8,128)(2,1)S(1)}, u32[]{:S(2)}, u32[]{:S(2)}) collective-permute-start(bf16[1,2,1,64,256]{4,3,2,1,0:T(8,128)(2,1)} %get-tuple-element.24), channel_id=1, source_target_pairs={{1,0},{2,1},{3,2},{0,3},{5,4},{6,5},{7,6},{4,7},{9,8},{10,9},{11,1... | collective-permute-start | bytes 196616 | tf_op jit(solution)/shard_map/ppermute | solution.py:28
  7.5 1.2 %fusion.25 = f32[2]{0:T(128)S(1)} fusion(bf16[2,4,64,256]{3,2,1,0:T(8,128)(2,1)} %param.4), kind=kLoop, calls=%fused_computation.49 | loop fusion | flops 786430 | bytes 262152 | tf_op jit(solution)/shard_map/reduce_sum | solution.py:115
  8.8 1.1 %fusion.54 = (f32[2,4,64,255]{3,2,1,0:T(8,128)}, f32[2,4,64,255]{3,2,1,0:T(8,128)}) fusion(bf16[2,4,64,256]{3,2,1,0:T(8,128)(2,1)S(1)} %copy-done), kind=kLoop, calls=%fused_computation.103 | loop fusion | bytes 2088960 | tf_op jit(solution)/shard_map/jit(_roll_static)/slice | solution.py:142
  9.9 0.8 %fusion.53 = (f32[2,4,64,1]{3,2,1,0:T(8,128)}, f32[2,4,64,1]{3,2,1,0:T(8,128)}) fusion(bf16[2,4,64,256]{3,2,1,0:T(8,128)(2,1)S(1)} %copy-done), kind=kLoop, calls=%fused_computation.102 | loop fusion | bytes 8192 | tf_op jit(solution)/shard_map/jit(_roll_static)/slice | solution.py:142
  11.4 6.3 %psum.14 = f32[2]{0:T(128)S(1)} all-reduce(f32[2]{0:T(128)S(1)} %fusion.25), channel_id=1, replica_groups=mesh['grp'=2,'img'=4,'gz'=4] {'gz'}, use_global_device_ids=true, to_apply=%region_1.0 | all-reduce | flops 2 | bytes 16 | tf_op jit(solution)/shard_map/psum | solution.py:116
  17.7 0.6 %broadcast_multiply_fusion = f32[2]{0:T(128)} fusion(f32[2]{0:T(128)S(1)} %psum.14, f32[]{:T(128)S(6)} %mul.146), kind=kLoop, calls=%fused_computation.94 | loop fusion | flops 2 | bytes 20 | tf_op jit(solution)/shard_map/mul | solution.py:116
  18.9 1.3 %dynamic-slice = u32[1]{0:T(128)} dynamic-slice(u32[32]{0:T(128)} %constant.66, u32[]{:T(128)S(6)} %add.140), dynamic_slice_sizes={1} | dynamic-slice | bytes 12
  21.5 0.2 slice.341
  21.7 0.2 slice.310
  22.1 0.2 slice_subtract_fusion
  22.4 0.4 copy-done.6
  22.8 0.9 %fusion.3 = (f32[2,5,64,256]{3,2,1,0:T(8,128)S(1)}, f32[2,5,64,256]{3,2,1,0:T(8,128)S(1)}, f32[2,5,64,256]{3,2,1,0:T(8,128)S(1)}, f32[2,5,64,256]{3,2,1,0:T(8,128)S(1)}, f32[2,5,64,256]{3,2,1,0:T(8,128)S(1)}) fusion(f32[3,2,5,64,256]{4,3,2,1,0:T(8,128)S(1)} %slice_subtract_fusion, f32[2,5,64,1]{3,2,1,0:T(8,128)S(1)} %slice.342, ...), kind=kLoop, calls=%fused_computation.7 | loop fusion | flops 4096000 | bytes 10485772 | tf_op jit(solution)/shard_map/mul | solution.py:57
  23.7 0.4 multiply_add_fusion.1
  24.7 0.3 fusion.10
  25.3 0.8 %copy-done.2 = f32[2,4,64,255]{3,2,1,0:T(8,128)S(1)} copy-done((f32[2,4,64,255]{3,2,1,0:T(8,128)S(1)}, f32[2,4,64,255]{3,2,1,0:T(8,128)}, u32[]{:S(2)}) %copy-start.2) | copy-done | bytes 522264
  26.3 0.6 %fusion.41 = bf16[2,4,64,256]{3,2,1,0:T(8,128)(2,1)S(1)} fusion(f32[2,4,64,1]{3,2,1,0:T(8,128)S(1)} %copy-done.5, f32[2,4,64,255]{3,2,1,0:T(8,128)S(1)} %copy-done.3, f32[2,4,64,255]{3,2,1,0:T(8,128)S(1)} %copy-done.2, f32[2,4,64,1]{3,2,1,0:T(8,128)S(1)} %copy-done.4, f32[2,4,1,256]{3,2,1,0:T(1,128)S(1)} %get-tuple-element.26, ...), kind=kLoop, calls=%fused_computation.82 | loop fusion | flops 4063232 | bytes 4980744 | tf_op jit(solution)/shard_map/convert_element_type | solution.py:151
  27.0 3.6 %collective-permute-start.4 = (bf16[1,4,64,256]{3,2,1,0:T(8,128)(2,1)S(1)}, bf16[1,4,64,256]{3,2,1,0:T(8,128)(2,1)S(1)}, u32[]{:S(2)}, u32[]{:S(2)}) collective-permute-start(bf16[1,4,64,256]{3,2,1,0:T(8,128)(2,1)S(1)} %get-tuple-element.21), channel_id=1, source_target_pairs={{0,4},{4,8},{8,12},{1,5},{5,9},{9,13},{2,6},{6,10},{10,14},{3,7},{... | collective-permute-start | bytes 393224 | tf_op jit(solution)/shard_map/ppermute | solution.py:26
  30.6 1.3 %collective-permute-start.5 = (bf16[1,4,64,256]{3,2,1,0:T(8,128)(2,1)S(1)}, bf16[1,4,64,256]{3,2,1,0:T(8,128)(2,1)S(1)}, u32[]{:S(2)}, u32[]{:S(2)}) collective-permute-start(bf16[1,4,64,256]{3,2,1,0:T(8,128)(2,1)S(1)} %get-tuple-element.22), channel_id=1, source_target_pairs={{4,0},{8,4},{12,8},{5,1},{9,5},{13,9},{6,2},{10,6},{14,10},{7,3},{... | collective-permute-start | bytes 393224 | tf_op jit(solution)/shard_map/ppermute | solution.py:28
  31.9 0.7 %fusion.31 = (f32[1,2,4,64,256]{4,3,2,1,0:T(8,128)S(1)}, f32[1,2,4,64,256]{4,3,2,1,0:T(8,128)S(1)}) fusion(f32[2,5,64,256]{3,2,1,0:T(8,128)S(1)} %get-tuple-element.6, f32[2,4,63,256]{3,2,1,0:T(8,128)S(1)} %slice.324, f32[2,4,1,256]{3,2,1,0:T(1,128)S(1)} %slice.323, f32[2,4,64,255]{3,2,1,0:T(8,128)S(1)} %slice.331, f32[2,4,64,1]{3,2,1,0:T(8,128)S(1)} %slice.330, ...), kind=kLoop, calls=%fused_computation.58 | loop fusion | flops 1835008 | bytes 6815744 | tf_op jit(solution)/shard_map/stack | solution.py:129
  32.9 0.5 collective-permute-done.4
  33.4 4.1 %collective-permute-done.5 = bf16[1,4,64,256]{3,2,1,0:T(8,128)(2,1)S(1)} collective-permute-done((bf16[1,4,64,256]{3,2,1,0:T(8,128)(2,1)S(1)}, bf16[1,4,64,256]{3,2,1,0:T(8,128)(2,1)S(1)}, u32[]{:S(2)}, u32[]{:S(2)}) %collective-permute-start.5) | collective-permute-done | bytes 131104 | tf_op jit(solution)/shard_map/ppermute | solution.py:28
  37.8 0.4 fusion.27
  38.1 5.7 %psum.15 = f32[2]{0:T(128)S(1)} all-reduce(f32[2]{0:T(128)S(1)} %multiply_reduce_fusion), channel_id=1, replica_groups=mesh['grp'=2,'img'=4,'gz'=4] {'gz'}, use_global_device_ids=true, to_apply=%region_3.4 | all-reduce | flops 2 | bytes 16 | tf_op jit(solution)/shard_map/psum | solution.py:159
  43.9 1.1 %fusion.1 = bf16[3,2,4,64,256]{4,3,2,1,0:T(8,128)(2,1)} fusion(f32[1,2,4,64,256]{4,3,2,1,0:T(8,128)S(1)} %fusion.27, f32[1,2,4,64,256]{4,3,2,1,0:T(8,128)S(1)} %get-tuple-element.20, f32[1,2,4,64,256]{4,3,2,1,0:T(8,128)S(1)} %get-tuple-element.19, bf16[3,2,4,64,256]{4,3,2,1,0:T(8,128)(2,1)S(1)} %copy-done.1), kind=kLoop, calls=%fused_computation.3 | loop fusion | flops 2359296 | bytes 3145728 | tf_op jit(solution)/shard_map/convert_element_type | solution.py:136
  45.1 9.9 %all-reduce = f32[8]{0:T(128)S(1)} all-reduce(f32[8]{0:T(128)S(1)} %sqrt_dynamic-update-slice_fusion), channel_id=1, replica_groups=mesh['grp'=2,'img'=4,'gz'=4] {'img'}, use_global_device_ids=true, to_apply=%add | all-reduce | flops 8 | bytes 64
  55.2 0.6 %slice.265 = f32[1,1]{0,1:T(1,128)} slice(f32[7,1]{0,1:T(1,128)S(1)} %reduce-window.4), slice={[6:7], [0:1]} | slice | bytes 8 | tf_op jit(solution)/shard_map/slice | solution.py:167
  56.6 0.9 %fusion.34 = bf16[2,4,64,256]{3,2,1,0:T(8,128)(2,1)} fusion(f32[4,4,64,256]{3,2,1,0:T(8,128)S(1)} %maximum_convert_fusion.1, f32[2]{0:T(128)S(1)} %get-tuple-element.34, f32[2]{0:T(128)S(1)} %get-tuple-element.33), kind=kLoop, calls=%fused_computation.62 | loop fusion | flops 917504 | bytes 1835024 | tf_op jit(solution)/shard_map/convert_element_type | solution.py:179
  (54 shorter events, 2.8 us)
Async XLA Ops:
  0.6 8.1 %copy-start = (bf16[2,4,64,256]{3,2,1,0:T(8,128)(2,1)S(1)}, bf16[2,4,64,256]{3,2,1,0:T(8,128)(2,1)}, u32[]{:S(2)}) copy-start(bf16[2,4,64,256]{3,2,1,0:T(8,128)(2,1)} %param.4) | copy-start | bytes 786436
  1.7 19.3 %collective-permute-start.2 = (bf16[3,2,1,64,256]{4,3,2,1,0:T(8,128)(2,1)S(1)}, bf16[3,2,1,64,256]{4,3,2,1,0:T(8,128)(2,1)S(1)}, u32[]{:S(2)}, u32[]{:S(2)}) collective-permute-start(bf16[3,2,1,64,256]{4,3,2,1,0:T(8,128)(2,1)S(1)} %get-tuple-element.15), channel_id=1, source_target_pairs={{0,1},{1,2},{2,3},{3,0},{4,5},{5,6},{6,7},{7,4},{8,9},{9,10},{10,1... | collective-permute-start | bytes 589832 | tf_op jit(solution)/shard_map/ppermute | solution.py:26
  2.3 18.7 %collective-permute-start.3 = (bf16[3,2,1,64,256]{4,3,2,1,0:T(8,128)(2,1)S(1)}, bf16[3,2,1,64,256]{4,3,2,1,0:T(8,128)(2,1)S(1)}, u32[]{:S(2)}, u32[]{:S(2)}) collective-permute-start(bf16[3,2,1,64,256]{4,3,2,1,0:T(8,128)(2,1)S(1)} %get-tuple-element.16), channel_id=1, source_target_pairs={{1,0},{2,1},{3,2},{0,3},{5,4},{6,5},{7,6},{4,7},{9,8},{10,9},{11,1... | collective-permute-start | bytes 589832 | tf_op jit(solution)/shard_map/ppermute | solution.py:28
  5.8 15.1 %collective-permute-start = (bf16[1,2,1,64,256]{4,3,2,1,0:T(8,128)(2,1)}, bf16[1,2,1,64,256]{4,3,2,1,0:T(8,128)(2,1)S(1)}, u32[]{:S(2)}, u32[]{:S(2)}) collective-permute-start(bf16[1,2,1,64,256]{4,3,2,1,0:T(8,128)(2,1)} %get-tuple-element.23), channel_id=1, source_target_pairs={{0,1},{1,2},{2,3},{3,0},{4,5},{5,6},{6,7},{7,4},{8,9},{9,10},{10,1... | collective-permute-start | bytes 196616 | tf_op jit(solution)/shard_map/ppermute | solution.py:26
  6.4 14.5 %collective-permute-start.1 = (bf16[1,2,1,64,256]{4,3,2,1,0:T(8,128)(2,1)}, bf16[1,2,1,64,256]{4,3,2,1,0:T(8,128)(2,1)S(1)}, u32[]{:S(2)}, u32[]{:S(2)}) collective-permute-start(bf16[1,2,1,64,256]{4,3,2,1,0:T(8,128)(2,1)} %get-tuple-element.24), channel_id=1, source_target_pairs={{1,0},{2,1},{3,2},{0,3},{5,4},{6,5},{7,6},{4,7},{9,8},{10,9},{11,1... | collective-permute-start | bytes 196616 | tf_op jit(solution)/shard_map/ppermute | solution.py:28
  9.9 11.1 %copy-start.1 = (bf16[3,2,4,64,256]{4,3,2,1,0:T(8,128)(2,1)S(1)}, bf16[3,2,4,64,256]{4,3,2,1,0:T(8,128)(2,1)}, u32[]{:S(2)}) copy-start(bf16[3,2,4,64,256]{4,3,2,1,0:T(8,128)(2,1)} %param.5) | copy-start | bytes 2359300
  22.1 0.7 %copy-start.6 = (f32[2]{0:T(128)S(1)}, f32[2]{0:T(128)}, u32[]{:S(2)}) copy-start(f32[2]{0:T(128)} %broadcast_multiply_fusion) | copy-start | bytes 28
  25.0 1.0 %copy-start.2 = (f32[2,4,64,255]{3,2,1,0:T(8,128)S(1)}, f32[2,4,64,255]{3,2,1,0:T(8,128)}, u32[]{:S(2)}) copy-start(f32[2,4,64,255]{3,2,1,0:T(8,128)} %get-tuple-element.31) | copy-start | bytes 1566724
  25.0 1.2 %copy-start.3 = (f32[2,4,64,255]{3,2,1,0:T(8,128)S(1)}, f32[2,4,64,255]{3,2,1,0:T(8,128)}, u32[]{:S(2)}) copy-start(f32[2,4,64,255]{3,2,1,0:T(8,128)} %get-tuple-element.32) | copy-start | bytes 1566724
  25.0 1.2 %copy-start.4 = (f32[2,4,64,1]{3,2,1,0:T(8,128)S(1)}, f32[2,4,64,1]{3,2,1,0:T(8,128)}, u32[]{:S(2)}) copy-start(f32[2,4,64,1]{3,2,1,0:T(8,128)} %get-tuple-element.29) | copy-start | bytes 6148
  25.0 1.3 %copy-start.5 = (f32[2,4,64,1]{3,2,1,0:T(8,128)S(1)}, f32[2,4,64,1]{3,2,1,0:T(8,128)}, u32[]{:S(2)}) copy-start(f32[2,4,64,1]{3,2,1,0:T(8,128)} %get-tuple-element.30) | copy-start | bytes 6148
  27.0 6.4 %collective-permute-start.4 = (bf16[1,4,64,256]{3,2,1,0:T(8,128)(2,1)S(1)}, bf16[1,4,64,256]{3,2,1,0:T(8,128)(2,1)S(1)}, u32[]{:S(2)}, u32[]{:S(2)}) collective-permute-start(bf16[1,4,64,256]{3,2,1,0:T(8,128)(2,1)S(1)} %get-tuple-element.21), channel_id=1, source_target_pairs={{0,4},{4,8},{8,12},{1,5},{5,9},{9,13},{2,6},{6,10},{10,14},{3,7},{... | collective-permute-start | bytes 393224 | tf_op jit(solution)/shard_map/ppermute | solution.py:26
  30.6 6.9 %collective-permute-start.5 = (bf16[1,4,64,256]{3,2,1,0:T(8,128)(2,1)S(1)}, bf16[1,4,64,256]{3,2,1,0:T(8,128)(2,1)S(1)}, u32[]{:S(2)}, u32[]{:S(2)}) collective-permute-start(bf16[1,4,64,256]{3,2,1,0:T(8,128)(2,1)S(1)} %get-tuple-element.22), channel_id=1, source_target_pairs={{4,0},{8,4},{12,8},{5,1},{9,5},{13,9},{6,2},{10,6},{14,10},{7,3},{... | collective-permute-start | bytes 393224 | tf_op jit(solution)/shard_map/ppermute | solution.py:28
where the time goes:
time: 57.9 us; the launch traced here: 57.5 us
  blocking collectives  21.9 us (38%)
  local copies, waits for them, and re-layouts  9.9 us (17%)
  starting transfers between devices  9.19 us (16%)
  other arithmetic  8.32 us (14%)
  waiting for transfers between devices  4.63 us (8%)
  between operations  3.59 us (6%)
    unnamed x1, blocking collectives  9.92 us
    psum x1, blocking collectives, shards(): homogeneous = misfit_value * (lax.psum(partial_h, 'gz') / cells)  6.27 us
    psum x1, blocking collectives, shards(): squares = lax.psum(local_squares, 'gz')  5.67 us
    ppermute x3, starting transfers between devices, padded(): lax.ppermute(tail, axis, [(i, (i + 1) % count) for i in range(ends)])  4.79 us
    ppermute x3, starting transfers between devices, padded(): lax.ppermute(head, axis, [((i + 1) % count, i) for i in range(ends)])  4.4 us
    ppermute x3, waiting for transfers between devices, padded(): lax.ppermute(head, axis, [((i + 1) % count, i) for i in range(ends)])  4.13 us
    unnamed x16, local copies, waits for them, and re-layouts  2.81 us
    slice x3, local copies, waits for them, and re-layouts, padded(): lax.slice_in_dim(cells, cells.shape[dim] - width, cells.shape[dim], axis=...  2.65 us
  transfers between devices with their start and end apart: 6, of which 2 were waited for; matrix products, arithmetic and copies ran while one was open for 13% of the time, Pallas kernels for 0%

commit v1 on v0

v1 whole, which is shorter than its diff:
```python
import functools

import jax
import jax.numpy as jnp
from jax import lax
from jax.experimental import pallas as pl
from jax.experimental.pallas import tpu as pltpu
from jax.sharding import PartitionSpec as P

stiff_eleven = 2.5
stiff_twelve = 1.5
stiff_shear = 1.2
barrier_height = 1.0
latent_enthalpy = 8.0
dissolution_limit_kelvin = 1250.0
gradient_coef = 1.0
mobility = 0.1
elastic_step = 0.03
epsilon = 1e-06
LANES = 128
MESH = pl.DeviceIdType.MESH


def switching(value):
    return value * value * (3.0 - 2.0 * value)


def roll(field, shift, axis):
    return pltpu.roll(field, shift % field.shape[axis], axis)


def ahead_of(field, axis):
    return roll(field, -1, axis) - field


def behind_of(field, axis):
    return field - roll(field, 1, axis)


def lane_row(field):
    row = jnp.sum(field, axis=0, keepdims=True)
    out = row[:, :LANES]
    for start in range(LANES, row.shape[1], LANES):
        out = out + row[:, start : start + LANES]
    return out


def kernel(
    n_img,
    n_gz,
    misfit_ref,
    kelvin_ref,
    order_in,
    shift_in,
    string_ref,
    moved_ref,
    obuf,
    sbuf,
    rbuf,
    hbuf,
    gbuf,
    load_sem,
    halo_send,
    halo_recv,
    image_send,
    image_recv,
    h_send,
    h_recv,
    g_send,
    g_recv,
):
    images, planes, nx, ny = order_in.shape
    cells = float(planes * n_gz * nx * ny)
    img = lax.axis_index("img")
    gz = lax.axis_index("gz")
    n_all = n_img * n_gz
    me = img * n_gz + gz
    above, below = lax.rem(gz + 1, n_gz), lax.rem(gz + n_gz - 1, n_gz)

    loads = [
        pltpu.make_async_copy(order_in, obuf.at[:, 1 : planes + 1], load_sem.at[0]),
        pltpu.make_async_copy(shift_in, sbuf.at[:, :, 1 : planes + 1], load_sem.at[1]),
    ]
    for load in loads:
        load.start()

    barrier = pltpu.get_barrier_semaphore()

    def greet(step, carry):
        other = lax.rem(me + step, n_all)
        pl.semaphore_signal(
            barrier,
            inc=1,
            device_id={"img": other // n_gz, "gz": lax.rem(other, n_gz)},
            device_id_type=MESH,
        )
        return carry

    lax.fori_loop(1, n_all, greet, 0)
    pl.semaphore_wait(barrier, n_all - 1)

    def halo(slot, source, target, neighbour):
        return pltpu.make_async_remote_copy(
            src_ref=source,
            dst_ref=target,
            send_sem=halo_send.at[slot],
            recv_sem=halo_recv.at[slot],
            device_id={"gz": neighbour},
            device_id_type=MESH,
        )

    last, top = planes - 1, planes + 1
    order_down = halo(0, order_in.at[:, 0], obuf.at[:, top], below)
    order_up = halo(1, order_in.at[:, last], obuf.at[:, 0], above)
    lift_down = halo(2, shift_in.at[2, :, 0], sbuf.at[2, :, top], below)
    shift_up = halo(3, shift_in.at[:, :, last], sbuf.at[:, :, 0], above)
    flat_down = halo(4, shift_in.at[0:2, :, 0], sbuf.at[0:2, :, top], below)
    first_halos = (order_down, order_up, lift_down)
    later_halos = (shift_up, flat_down)
    for copy in first_halos + later_halos:
        copy.start()

    misfit = misfit_ref[0]
    drive = latent_enthalpy * (kelvin_ref[0] - dissolution_limit_kelvin) / dissolution_limit_kelvin

    def order_at(l, z):
        return obuf[l, z].astype(jnp.float32)

    def shift_at(c, l, z):
        return sbuf[c, l, z].astype(jnp.float32)

    loads[0].wait()
    for l in range(images):

        def add_h(z, total, l=l):
            return total + lane_row(switching(order_at(l, z + 1)))

        hbuf[gz, l : l + 1] = lax.fori_loop(0, planes, add_h, jnp.zeros((1, LANES), jnp.float32))

    def h_copy(step):
        return pltpu.make_async_remote_copy(
            src_ref=hbuf.at[gz],
            dst_ref=hbuf.at[gz],
            send_sem=h_send.at[step],
            recv_sem=h_recv.at[step],
            device_id={"gz": lax.rem(gz + step, n_gz)},
            device_id_type=MESH,
        )

    def h_arrival(step):
        origin = lax.rem(gz + n_gz - step, n_gz)
        return pltpu.make_async_remote_copy(
            src_ref=hbuf.at[origin],
            dst_ref=hbuf.at[origin],
            send_sem=h_send.at[step],
            recv_sem=h_recv.at[step],
            device_id={"gz": origin},
            device_id_type=MESH,
        )

    for step in range(1, n_gz):
        h_copy(step).start()

    def move_plane(l, z):
        ux, uy, uz = shift_at(0, l, z + 1), shift_at(1, l, z + 1), shift_at(2, l, z + 1)
        vx, vy, vz = shift_at(0, l, z), shift_at(1, l, z), shift_at(2, l, z)
        zx = shift_at(0, l, z + 2) - ux
        zy = shift_at(1, l, z + 2) - uy
        zz = shift_at(2, l, z + 2) - uz
        dx, dy, dz = ux - vx, uy - vy, uz - vz
        total = stiff_eleven + 2.0 * stiff_twelve
        swell = (-total * misfit) * switching(order_at(l, z + 1))
        swell_under = (-total * misfit) * switching(order_at(l, z))
        xx, yy = ahead_of(ux, 0), ahead_of(uy, 1)
        s_xx = stiff_eleven * xx + stiff_twelve * (yy + zz) + swell
        s_yy = stiff_eleven * yy + stiff_twelve * (xx + zz) + swell
        s_xy = stiff_shear * (ahead_of(uy, 0) + ahead_of(ux, 1))
        s_xz = stiff_shear * (ahead_of(uz, 0) + zx)
        s_yz = stiff_shear * (ahead_of(uz, 1) + zy)
        f_x = behind_of(s_xx, 0) + behind_of(s_xy, 1)
        f_x = f_x + stiff_shear * (ahead_of(dz, 0) + (zx - dx))
        moved_ref[0, l, z] = (ux + elastic_step * f_x).astype(jnp.bfloat16)
        f_y = behind_of(s_xy, 0) + behind_of(s_yy, 1)
        f_y = f_y + stiff_shear * (ahead_of(dz, 1) + (zy - dy))
        moved_ref[1, l, z] = (uy + elastic_step * f_y).astype(jnp.bfloat16)
        f_z = behind_of(s_xz, 0) + behind_of(s_yz, 1)
        f_z = f_z + stiff_eleven * (zz - dz)
        f_z = f_z + stiff_twelve * (ahead_of(dx, 0) + ahead_of(dy, 1)) + (swell - swell_under)
        moved_ref[2, l, z] = (uz + elastic_step * f_z).astype(jnp.bfloat16)

    def relax_plane(l, z, homogeneous):
        order = order_at(l, z + 1)
        uz = shift_at(2, l, z + 1)
        divergence = ahead_of(shift_at(0, l, z + 1), 0) + ahead_of(shift_at(1, l, z + 1), 1)
        divergence = divergence + (shift_at(2, l, z + 2) - uz)
        eigen = homogeneous - misfit * switching(order)
        trace = (stiff_eleven + 2.0 * stiff_twelve) * (divergence + 3.0 * eigen)
        laplace = order_at(l, z) + order_at(l, z + 2)
        laplace = laplace + (roll(order, 1, 0) + roll(order, -1, 0))
        laplace = laplace + (roll(order, 1, 1) + roll(order, -1, 1)) - 6.0 * order
        bend = order * (1.0 - order)
        potential = (
            bend * (barrier_height * 2.0 * (1.0 - 2.0 * order) + 6.0 * (drive - misfit * trace))
            - gradient_coef * laplace
        )
        rbuf[l + 1, z] = (order - mobility * potential).astype(jnp.bfloat16)

    inner = planes - 2

    def inner_planes(work):
        def one(step, carry):
            work(step // inner, lax.rem(step, inner) + 1)
            return carry

        lax.fori_loop(0, images * inner, one, 0)

    def outer_planes(work):
        def one(step, carry):
            work(step // 2, lax.rem(step, 2) * last)
            return carry

        lax.fori_loop(0, images * 2, one, 0)

    loads[1].wait()
    inner_planes(move_plane)

    for step in range(1, n_gz):
        h_arrival(step).wait_recv()
    h_sum = jnp.sum(jnp.sum(hbuf[...], axis=0), axis=-1, keepdims=True)
    h_mean = misfit * (h_sum / cells)

    def relax(l, z):
        picked = jnp.where(lax.broadcasted_iota(jnp.int32, (images, 1), 0) == l, h_mean, 0.0)
        relax_plane(l, z, jnp.sum(picked, axis=0, keepdims=True))

    inner_planes(relax)

    has_next = img < n_img - 1
    has_previous = img > 0

    def image_copy(slot, span, forward):
        return pltpu.make_async_remote_copy(
            src_ref=rbuf.at[images if forward else 1, span],
            dst_ref=rbuf.at[0 if forward else images + 1, span],
            send_sem=image_send.at[slot],
            recv_sem=image_recv.at[slot],
            device_id={"img": img + 1 if forward else img - 1},
            device_id_type=MESH,
        )

    spans = (slice(1, last), slice(0, 1), slice(last, planes))
    forward_copies = [image_copy(i, span, True) for i, span in enumerate(spans)]
    backward_copies = [image_copy(3 + i, span, False) for i, span in enumerate(spans)]

    def send_images(picks):
        @pl.when(has_previous)
        def _():
            for i in picks:
                backward_copies[i].start()

        @pl.when(has_next)
        def _():
            for i in picks:
                forward_copies[i].start()

    send_images((0,))

    @pl.when(jnp.logical_not(has_previous))
    def _():
        rbuf[0] = jnp.zeros_like(rbuf[0])

    @pl.when(jnp.logical_not(has_next))
    def _():
        rbuf[images + 1] = jnp.zeros_like(rbuf[images + 1])

    for copy in first_halos:
        copy.wait_recv()
    outer_planes(relax)
    send_images((1, 2))

    def squares(l):
        def add(z, total):
            step = rbuf[l + 2, z].astype(jnp.float32) - rbuf[l + 1, z].astype(jnp.float32)
            return total + lane_row(step * step)

        gbuf[me, l : l + 1] = lax.fori_loop(0, planes, add, jnp.zeros((1, LANES), jnp.float32))

    for l in range(images - 1):
        squares(l)

    @pl.when(has_next)
    def _():
        for copy in backward_copies:
            copy.wait_recv()

    squares(images - 1)

    def place(index):
        return {"img": index // n_gz, "gz": lax.rem(index, n_gz)}

    def g_copy(step):
        return pltpu.make_async_remote_copy(
            src_ref=gbuf.at[me],
            dst_ref=gbuf.at[me],
            send_sem=g_send.at[step],
            recv_sem=g_recv.at[step],
            device_id=place(lax.rem(me + step, n_all)),
            device_id_type=MESH,
        )

    def g_arrival(step):
        origin = lax.rem(me + n_all - step, n_all)
        return pltpu.make_async_remote_copy(
            src_ref=gbuf.at[origin],
            dst_ref=gbuf.at[origin],
            send_sem=g_send.at[step],
            recv_sem=g_recv.at[step],
            device_id=place(origin),
            device_id_type=MESH,
        )

    def g_start(step, carry):
        g_copy(step).start()
        return carry

    lax.fori_loop(1, n_all, g_start, 0)

    for copy in later_halos:
        copy.wait_recv()
    outer_planes(move_plane)

    @pl.when(has_previous)
    def _():
        for copy in forward_copies:
            copy.wait_recv()

    def g_wait(step, carry):
        g_arrival(step).wait_recv()
        return carry

    lax.fori_loop(1, n_all, g_wait, 0)

    total_images = images * n_img
    gaps = []
    for i in range(n_img):
        part = jnp.sum(gbuf[i * n_gz : (i + 1) * n_gz], axis=0)
        part = jnp.sum(part, axis=-1, keepdims=True)
        gaps.append(jnp.sqrt(part / cells + epsilon))

    def pick(low, high):
        out = jnp.zeros((1, 1), jnp.float32)
        for i in range(n_img):
            row = lax.broadcasted_iota(jnp.int32, (images, 1), 0) + i * images
            chosen = jnp.where((row >= low) & (row < high), gaps[i], 0.0)
            out = out + jnp.sum(chosen, axis=0, keepdims=True)
        return out

    length = pick(0, total_images - 1)
    for l in range(images):
        position = img * images + l
        arc = pick(0, position)
        target = length * (position.astype(jnp.float32) / (total_images - 1))
        gap_under = jnp.where(position == 0, 1.0, pick(position - 1, position))
        gap_over = jnp.where(position == total_images - 1, 1.0, pick(position, position + 1))
        back = jnp.clip((arc - target) / gap_under, 0.0, 1.0)
        ahead = jnp.clip((target - arc) / gap_over, 0.0, 1.0)

        def blend(z, carry, l=l, back=back, ahead=ahead):
            current = rbuf[l + 1, z].astype(jnp.float32)
            following = rbuf[l + 2, z].astype(jnp.float32)
            previous = rbuf[l, z].astype(jnp.float32)
            string_ref[l, z] = (
                current + ahead * (following - current) + back * (previous - current)
            ).astype(jnp.bfloat16)
            return carry

        lax.fori_loop(0, planes, blend, 0)

    for copy in first_halos + later_halos:
        copy.wait_send()
    for step in range(1, n_gz):
        h_copy(step).wait_send()

    @pl.when(has_previous)
    def _():
        for copy in backward_copies:
            copy.wait_send()

    @pl.when(has_next)
    def _():
        for copy in forward_copies:
            copy.wait_send()

    def g_done(step, carry):
        g_copy(step).wait_send()
        return carry

    lax.fori_loop(1, n_all, g_done, 0)


def shards(ordering_variable, lattice_shift_field, eigenstrain_mismatch, thermal_state_kelvin):
    n_img, n_gz = lax.axis_size("img"), lax.axis_size("gz")
    images, planes, nx, ny = ordering_variable.shape
    dma = pltpu.SemaphoreType.DMA
    return pl.pallas_call(
        functools.partial(kernel, n_img, n_gz),
        out_shape=(
            jax.ShapeDtypeStruct(ordering_variable.shape, jnp.bfloat16),
            jax.ShapeDtypeStruct(lattice_shift_field.shape, jnp.bfloat16),
        ),
        in_specs=[
            pl.BlockSpec(memory_space=pltpu.SMEM),
            pl.BlockSpec(memory_space=pltpu.SMEM),
            pl.BlockSpec(memory_space=pl.ANY),
            pl.BlockSpec(memory_space=pl.ANY),
        ],
        out_specs=(
            pl.BlockSpec(memory_space=pltpu.VMEM),
            pl.BlockSpec(memory_space=pltpu.VMEM),
        ),
        scratch_shapes=[
            pltpu.VMEM((images, planes + 2, nx, ny), jnp.bfloat16),
            pltpu.VMEM((3, images, planes + 2, nx, ny), jnp.bfloat16),
            pltpu.VMEM((images + 2, planes, nx, ny), jnp.bfloat16),
            pltpu.VMEM((n_gz, images, LANES), jnp.float32),
            pltpu.VMEM((n_img * n_gz, images, LANES), jnp.float32),
            dma((2,)),
            dma((5,)),
            dma((5,)),
            dma((6,)),
            dma((6,)),
            dma((n_gz,)),
            dma((n_gz,)),
            dma((n_img * n_gz,)),
            dma((n_img * n_gz,)),
        ],
        compiler_params=pltpu.CompilerParams(
            collective_id=0, has_side_effects=True, vmem_limit_bytes=24 * 1024 * 1024
        ),
    )(eigenstrain_mismatch, thermal_state_kelvin, ordering_variable, lattice_shift_field)


def solution(mesh):
    in_specs = (
        P(("grp", "img"), "gz", None, None),
        P(None, ("grp", "img"), "gz", None, None),
        P("grp"),
        P("grp"),
    )
    out_specs = (P(("grp", "img"), "gz", None, None), P(None, ("grp", "img"), "gz", None, None))
    return jax.shard_map(shards, mesh=mesh, in_specs=in_specs, out_specs=out_specs, check_vma=False)
```

time: 57.9 us -> 28.8 us (0.50)
  Pallas kernels: 0 us -> 23 us
  blocking collectives: 21.9 us -> 0 us
  starting transfers between devices: 9.19 us -> 0 us
  other arithmetic: 8.32 us -> 0 us
  local copies, waits for them, and re-layouts: 9.9 us -> 3.66 us
  waiting for transfers between devices: 4.63 us -> 0 us
  between operations: 3.59 us -> 1.94 us
    pallas_call x0 -> x1, Pallas kernels: none -> 23 us  [shards(): pl.pallas_call(functools.partial(kernel, n_img, n_gz), out_shape=(jax.Sha...]
    psum x2 -> x0, blocking collectives: 11.9 us -> none  [the longest x1 6.27 us: shards(): homogeneous = misfit_value * (lax.psum(partial_h, 'gz') / cells)]
    unnamed x1 -> x0, blocking collectives: 9.92 us -> none
    ppermute x6 -> x0, starting transfers between devices: 9.19 us -> none  [the longest x3 4.79 us: padded(): lax.ppermute(tail, axis, [(i, (i + 1) % count) for i in range(ends)])]
    slice x33 -> x0, local copies, waits for them, and re-layouts: 6.89 us -> none  [the longest x3 2.65 us: padded(): lax.slice_in_dim(cells, cells.shape[dim] - width, cells.shape[dim], axis=...]
    ppermute x6 -> x0, waiting for transfers between devices: 4.63 us -> none  [the longest x3 4.13 us: padded(): lax.ppermute(head, axis, [((i + 1) % count, i) for i in range(ends)])]
    convert_element_type x7 -> x0, other arithmetic: 3.06 us -> none  [the longest x1 1.14 us: shards(): moved = (shifts + elastic_step * force).astype(jnp.bfloat16)]
    mul x3 -> x0, other arithmetic: 1.82 us -> none  [the longest x1 0.92 us: cubic_stress(): stiff_shear * (slopes[7] + slopes[8])]
  transfers between devices with their start and end apart: 6 -> 0, of which waited for: 2 -> 0; matrix products, arithmetic and copies ran while one was open for 13% -> 0% of each run, Pallas kernels for 0% -> 0%
where the time goes in v1:
time: 28.8 us; the launch traced here: 28.6 us
  Pallas kernels  23 us (80%)
  local copies, waits for them, and re-layouts  3.66 us (13%)
  between operations  1.94 us (7%)
    pallas_call x1, Pallas kernels, shards(): pl.pallas_call(functools.partial(kernel, n_img, n_gz), out_shape=(jax.Sha...  23 us
    unnamed x6, local copies, waits for them, and re-layouts  3.66 us

profile of v1, /device:TPU:0, one launch (start us, length us, event | category | flops | bytes accessed | tf_op | source)
XLA Modules:
  0.0 28.6 jit_solution(15768618077659547329)
XLA Ops:
  1.9 0.0 copy-start
  1.9 1.1 %copy-done = bf16[3,2,4,64,256]{4,3,2,1,0:T(8,128)(2,1)S(1)} copy-done((bf16[3,2,4,64,256]{4,3,2,1,0:T(8,128)(2,1)S(1)}, bf16[3,2,4,64,256]{4,3,2,1,0:T(8,128)(2,1)}, u32[]{:S(2)}) %copy-start) | copy-done | bytes 786456
  3.1 0.0 copy-start.1
  3.1 0.9 %copy-done.1 = bf16[2,4,64,256]{3,2,1,0:T(8,128)(2,1)S(1)} copy-done((bf16[2,4,64,256]{3,2,1,0:T(8,128)(2,1)S(1)}, bf16[2,4,64,256]{3,2,1,0:T(8,128)(2,1)}, u32[]{:S(2)}) %copy-start.1) | copy-done | bytes 262168
  4.0 23.0 %shard_map.59 = (bf16[2,4,64,256]{3,2,1,0:T(8,128)(2,1)S(1)}, bf16[3,2,4,64,256]{4,3,2,1,0:T(8,128)(2,1)S(1)}) custom-call(f32[1]{0:T(128)S(6)} %copy.8.misfit_ref, f32[1]{0:T(128)S(6)} %copy.9.kelvin_ref, bf16[2,4,64,256]{3,2,1,0:T(8,128)(2,1)S(1)} %copy-done.1, bf16[3,2,4,64,256]{4,3,2,1,0:T(8,128)(2,1)S(1)} %copy-done), custom_call_target="tpu_custom_call" | custom-call | tf_op jit(solution)/shard_map/pallas_call | solution.py:405
  27.0 0.7 %copy.10 = bf16[2,4,64,256]{3,2,1,0:T(8,128)(2,1)} copy(bf16[2,4,64,256]{3,2,1,0:T(8,128)(2,1)S(1)} %get-tuple-element.4) | data formatting | bytes 524288
  27.7 0.9 %copy.11 = bf16[3,2,4,64,256]{4,3,2,1,0:T(8,128)(2,1)} copy(bf16[3,2,4,64,256]{4,3,2,1,0:T(8,128)(2,1)S(1)} %get-tuple-element.5) | data formatting | bytes 1572864
Async XLA Ops:
  1.9 1.1 %copy-start = (bf16[3,2,4,64,256]{4,3,2,1,0:T(8,128)(2,1)S(1)}, bf16[3,2,4,64,256]{4,3,2,1,0:T(8,128)(2,1)}, u32[]{:S(2)}) copy-start(bf16[3,2,4,64,256]{4,3,2,1,0:T(8,128)(2,1)} %shift_in.1) | copy-start | bytes 2359300
  3.1 0.9 %copy-start.1 = (bf16[2,4,64,256]{3,2,1,0:T(8,128)(2,1)S(1)}, bf16[2,4,64,256]{3,2,1,0:T(8,128)(2,1)}, u32[]{:S(2)}) copy-start(bf16[2,4,64,256]{3,2,1,0:T(8,128)(2,1)} %order_in.1) | copy-start | bytes 786436

commit v2 on v1

--- a/solution.py
+++ b/solution.py
@@ -52,13 +52,14 @@
     kelvin_ref,
     order_in,
     shift_in,
-    string_ref,
+    rbuf,
     moved_ref,
+    weight_ref,
     obuf,
     sbuf,
-    rbuf,
     hbuf,
     gbuf,
+    word_sem,
     load_sem,
     halo_send,
     halo_recv,
@@ -86,18 +87,35 @@
 
     barrier = pltpu.get_barrier_semaphore()
 
-    def greet(step, carry):
-        other = lax.rem(me + step, n_all)
+    has_next = img < n_img - 1
+    has_previous = img > 0
+    n_near = has_next.astype(jnp.int32) + has_previous.astype(jnp.int32)
+
+    def signal_near(sem):
+        @pl.when(has_next)
+        def _():
+            pl.semaphore_signal(sem, inc=1, device_id={"img": img + 1}, device_id_type=MESH)
+
+        @pl.when(has_previous)
+        def _():
+            pl.semaphore_signal(sem, inc=1, device_id={"img": img - 1}, device_id_type=MESH)
+
+    for step in range(1, n_gz):
         pl.semaphore_signal(
             barrier,
             inc=1,
-            device_id={"img": other // n_gz, "gz": lax.rem(other, n_gz)},
-            device_id_type=MESH,
-        )
-        return carry
-
-    lax.fori_loop(1, n_all, greet, 0)
-    pl.semaphore_wait(barrier, n_all - 1)
+            device_id={"gz": lax.rem(gz + step, n_gz)},
+            device_id_type=MESH,
+        )
+    signal_near(barrier)
+    pl.semaphore_wait(barrier, n_gz - 1 + n_near)
+
+    def spread(first, stop):
+        for stage in range(first, stop):
+            if stage > 0:
+                pl.semaphore_wait(word_sem.at[stage - 1], n_near)
+            if stage < n_img - 1:
+                signal_near(word_sem.at[stage])
 
     def halo(slot, source, target, neighbour):
         return pltpu.make_async_remote_copy(
@@ -117,8 +135,9 @@
     flat_down = halo(4, shift_in.at[0:2, :, 0], sbuf.at[0:2, :, top], below)
     first_halos = (order_down, order_up, lift_down)
     later_halos = (shift_up, flat_down)
-    for copy in first_halos + later_halos:
+    for copy in first_halos:
         copy.start()
+    spread(0, 1)
 
     misfit = misfit_ref[0]
     drive = latent_enthalpy * (kelvin_ref[0] - dissolution_limit_kelvin) / dissolution_limit_kelvin
@@ -160,6 +179,7 @@
 
     for step in range(1, n_gz):
         h_copy(step).start()
+    spread(1, 2)
 
     def move_plane(l, z):
         ux, uy, uz = shift_at(0, l, z + 1), shift_at(1, l, z + 1), shift_at(2, l, z + 1)
@@ -222,7 +242,7 @@
         lax.fori_loop(0, images * 2, one, 0)
 
     loads[1].wait()
-    inner_planes(move_plane)
+    spread(2, 3)
 
     for step in range(1, n_gz):
         h_arrival(step).wait_recv()
@@ -230,13 +250,16 @@
     h_mean = misfit * (h_sum / cells)
 
     def relax(l, z):
-        picked = jnp.where(lax.broadcasted_iota(jnp.int32, (images, 1), 0) == l, h_mean, 0.0)
-        relax_plane(l, z, jnp.sum(picked, axis=0, keepdims=True))
-
-    inner_planes(relax)
-
-    has_next = img < n_img - 1
-    has_previous = img > 0
+        relax_plane(l, z, h_mean[l : l + 1])
+
+    for l in range(images):
+
+        def relax_inner(z, carry, l=l):
+            relax(l, z)
+            return carry
+
+        lax.fori_loop(1, last, relax_inner, 0)
+    spread(3, n_img)
 
     def image_copy(slot, span, forward):
         return pltpu.make_async_remote_copy(
@@ -273,27 +296,42 @@
     def _():
         rbuf[images + 1] = jnp.zeros_like(rbuf[images + 1])
 
-    for copy in first_halos:
-        copy.wait_recv()
-    outer_planes(relax)
-    send_images((1, 2))
-
-    def squares(l):
+    inner_planes(move_plane)
+
+    order_up.wait_recv()
+    for l in range(images):
+        relax(l, 0)
+    send_images((1,))
+    order_down.wait_recv()
+    lift_down.wait_recv()
+    for copy in later_halos:
+        copy.start()
+    for l in range(images):
+        relax(l, last)
+    send_images((2,))
+
+    def squares(l, first, stop, total):
         def add(z, total):
             step = rbuf[l + 2, z].astype(jnp.float32) - rbuf[l + 1, z].astype(jnp.float32)
             return total + lane_row(step * step)
 
-        gbuf[me, l : l + 1] = lax.fori_loop(0, planes, add, jnp.zeros((1, LANES), jnp.float32))
-
+        return lax.fori_loop(first, stop, add, total)
+
+    nothing = jnp.zeros((1, LANES), jnp.float32)
     for l in range(images - 1):
-        squares(l)
-
-    @pl.when(has_next)
-    def _():
-        for copy in backward_copies:
-            copy.wait_recv()
-
-    squares(images - 1)
+        gbuf[me, l : l + 1] = squares(l, 0, planes, nothing)
+
+    def await_following(picks):
+        @pl.when(has_next)
+        def _():
+            for i in picks:
+                backward_copies[i].wait_recv()
+
+    await_following((0,))
+    total = squares(images - 1, 1, last, nothing)
+    await_following((1, 2))
+    total = squares(images - 1, 0, 1, total)
+    gbuf[me, images - 1 : images] = squares(images - 1, last, planes, total)
 
     def place(index):
         return {"img": index // n_gz, "gz": lax.rem(index, n_gz)}
@@ -323,7 +361,7 @@
         g_copy(step).start()
         return carry
 
-    lax.fori_loop(1, n_all, g_start, 0)
+    lax.fori_loop(1, n_all, g_start, 0, unroll=n_all <= 32)
 
     for copy in later_halos:
         copy.wait_recv()
@@ -338,7 +376,7 @@
         g_arrival(step).wait_recv()
         return carry
 
-    lax.fori_loop(1, n_all, g_wait, 0)
+    lax.fori_loop(1, n_all, g_wait, 0, unroll=n_all <= 32)
 
     total_images = images * n_img
     gaps = []
@@ -364,17 +402,8 @@
         gap_over = jnp.where(position == total_images - 1, 1.0, pick(position, position + 1))
         back = jnp.clip((arc - target) / gap_under, 0.0, 1.0)
         ahead = jnp.clip((target - arc) / gap_over, 0.0, 1.0)
-
-        def blend(z, carry, l=l, back=back, ahead=ahead):
-            current = rbuf[l + 1, z].astype(jnp.float32)
-            following = rbuf[l + 2, z].astype(jnp.float32)
-            previous = rbuf[l, z].astype(jnp.float32)
-            string_ref[l, z] = (
-                current + ahead * (following - current) + back * (previous - current)
-            ).astype(jnp.bfloat16)
-            return carry
-
-        lax.fori_loop(0, planes, blend, 0)
+        weight_ref[l : l + 1] = jnp.broadcast_to(back, (1, ny))
+        weight_ref[images + l : images + l + 1] = jnp.broadcast_to(ahead, (1, ny))
 
     for copy in first_halos + later_halos:
         copy.wait_send()
@@ -395,35 +424,59 @@
         g_copy(step).wait_send()
         return carry
 
-    lax.fori_loop(1, n_all, g_done, 0)
+    lax.fori_loop(1, n_all, g_done, 0, unroll=n_all <= 32)
+
+
+def finish(relaxed_ref, moved_ref, weight_ref, string_out, moved_out, string_buf, sem):
+    images, planes = string_buf.shape[:2]
+    moved_copy = pltpu.make_async_copy(moved_ref, moved_out, sem.at[images])
+    moved_copy.start()
+    copies = []
+    for l in range(images):
+        back, ahead = weight_ref[l : l + 1], weight_ref[images + l : images + l + 1]
+
+        def blend(z, carry, l=l, back=back, ahead=ahead):
+            current = relaxed_ref[l + 1, z].astype(jnp.float32)
+            following = relaxed_ref[l + 2, z].astype(jnp.float32)
+            previous = relaxed_ref[l, z].astype(jnp.float32)
+            string_buf[l, z] = (
+                current + ahead * (following - current) + back * (previous - current)
+            ).astype(jnp.bfloat16)
+            return carry
+
+        lax.fori_loop(0, planes, blend, 0)
+        copies.append(pltpu.make_async_copy(string_buf.at[l], string_out.at[l], sem.at[l]))
+        copies[-1].start()
+    for copy in copies + [moved_copy]:
+        copy.wait()
 
 
 def shards(ordering_variable, lattice_shift_field, eigenstrain_mismatch, thermal_state_kelvin):
     n_img, n_gz = lax.axis_size("img"), lax.axis_size("gz")
     images, planes, nx, ny = ordering_variable.shape
     dma = pltpu.SemaphoreType.DMA
-    return pl.pallas_call(
+    ordering_variable = pltpu.with_memory_space_constraint(ordering_variable, pltpu.HBM)
+    lattice_shift_field = pltpu.with_memory_space_constraint(lattice_shift_field, pltpu.HBM)
+    relaxed, moved, weights = pl.pallas_call(
         functools.partial(kernel, n_img, n_gz),
         out_shape=(
-            jax.ShapeDtypeStruct(ordering_variable.shape, jnp.bfloat16),
+            jax.ShapeDtypeStruct((images + 2, planes, nx, ny), jnp.bfloat16),
             jax.ShapeDtypeStruct(lattice_shift_field.shape, jnp.bfloat16),
+            jax.ShapeDtypeStruct((2 * images, ny), jnp.float32),
         ),
         in_specs=[
             pl.BlockSpec(memory_space=pltpu.SMEM),
             pl.BlockSpec(memory_space=pltpu.SMEM),
-            pl.BlockSpec(memory_space=pl.ANY),
-            pl.BlockSpec(memory_space=pl.ANY),
+            pl.BlockSpec(memory_space=pltpu.HBM),
+            pl.BlockSpec(memory_space=pltpu.HBM),
         ],
-        out_specs=(
-            pl.BlockSpec(memory_space=pltpu.VMEM),
-            pl.BlockSpec(memory_space=pltpu.VMEM),
-        ),
+        out_specs=(pl.BlockSpec(memory_space=pltpu.VMEM),) * 3,
         scratch_shapes=[
             pltpu.VMEM((images, planes + 2, nx, ny), jnp.bfloat16),
             pltpu.VMEM((3, images, planes + 2, nx, ny), jnp.bfloat16),
-            pltpu.VMEM((images + 2, planes, nx, ny), jnp.bfloat16),
             pltpu.VMEM((n_gz, images, LANES), jnp.float32),
             pltpu.VMEM((n_img * n_gz, images, LANES), jnp.float32),
+            pltpu.SemaphoreType.REGULAR((n_img - 1,)),
             dma((2,)),
             dma((5,)),
             dma((5,)),
@@ -438,6 +491,17 @@
             collective_id=0, has_side_effects=True, vmem_limit_bytes=24 * 1024 * 1024
         ),
     )(eigenstrain_mismatch, thermal_state_kelvin, ordering_variable, lattice_shift_field)
+    return pl.pallas_call(
+        finish,
+        out_shape=(
+            jax.ShapeDtypeStruct(ordering_variable.shape, jnp.bfloat16),
+            jax.ShapeDtypeStruct(lattice_shift_field.shape, jnp.bfloat16),
+        ),
+        in_specs=[pl.BlockSpec(memory_space=pltpu.VMEM)] * 3,
+        out_specs=(pl.BlockSpec(memory_space=pltpu.HBM),) * 2,
+        scratch_shapes=[pltpu.VMEM(ordering_variable.shape, jnp.bfloat16), dma((images + 1,))],
+        compiler_params=pltpu.CompilerParams(vmem_limit_bytes=24 * 1024 * 1024),
+    )(relaxed, moved, weights)
 
 
 def solution(mesh):

time: 28.8 us -> 22 us (0.76)
  local copies, waits for them, and re-layouts: 3.66 us -> 0 us
  Pallas kernels: 23 us -> 20 us
    pallas_call x1, Pallas kernels: 23 us -> 19 us  [shards(): pl.pallas_call(functools.partial(kernel, n_img, n_gz), out_shape=(jax.Sha...]
    unnamed x6 -> x0, local copies, waits for them, and re-layouts: 3.66 us -> none
    pallas_call x0 -> x1, Pallas kernels: none -> 0.99 us  [shards(): pl.pallas_call(finish, out_shape=(jax.ShapeDtypeStruct(ordering_variable....]
where the time goes in v2:
time: 22 us; the launch traced here: 21.9 us
  Pallas kernels  20 us (91%)
  between operations  1.93 us (9%)
    pallas_call x1, Pallas kernels, shards(): pl.pallas_call(functools.partial(kernel, n_img, n_gz), out_shape=(jax.Sha...  19 us
    pallas_call x1, Pallas kernels, shards(): pl.pallas_call(finish, out_shape=(jax.ShapeDtypeStruct(ordering_variable....  0.99 us

profile of v2, /device:TPU:0, one launch (start us, length us, event | category | flops | bytes accessed | tf_op | source)
XLA Modules:
  0.0 21.9 jit_solution(11050594565434009138)
XLA Ops:
  1.9 19.0 %shard_map.59 = (bf16[4,4,64,256]{3,2,1,0:T(8,128)(2,1)S(1)}, bf16[3,2,4,64,256]{4,3,2,1,0:T(8,128)(2,1)S(1)}, f32[4,256]{1,0:T(4,128)S(1)}) custom-call(f32[1]{0:T(128)S(6)} %copy.6.misfit_ref, f32[1]{0:T(128)S(6)} %copy.7.kelvin_ref, bf16[2,4,64,256]{3,2,1,0:T(8,128)(2,1)} %order_in.1, bf16[3,2,4,64,256]{4,3,2,1,0:T(8,128)(2,1)} %shift_in.1), custom_call_target="tpu_custom_call" | custom-call | tf_op jit(solution)/shard_map/pallas_call | solution.py:460
  20.9 1.0 %shard_map.60 = (bf16[2,4,64,256]{3,2,1,0:T(8,128)(2,1)}, bf16[3,2,4,64,256]{4,3,2,1,0:T(8,128)(2,1)}) custom-call(bf16[4,4,64,256]{3,2,1,0:T(8,128)(2,1)S(1)} %get-tuple-element.5.relaxed_ref, bf16[3,2,4,64,256]{4,3,2,1,0:T(8,128)(2,1)S(1)} %get-tuple-element.6.moved_ref, f32[4,256]{1,0:T(4,128)S(1)} %get-tuple-element.7.weight_ref), custom_call_target="tpu_custom_call" | custom-call | tf_op jit(solution)/shard_map/pallas_call | solution.py:494

commit v3 on v2

--- a/solution.py
+++ b/solution.py
@@ -76,14 +76,19 @@
     gz = lax.axis_index("gz")
     n_all = n_img * n_gz
     me = img * n_gz + gz
-    above, below = lax.rem(gz + 1, n_gz), lax.rem(gz + n_gz - 1, n_gz)
+
+    def wrapped(index, count):
+        return jnp.where(index >= count, index - count, index)
+
+    gz_at = [wrapped(gz + step, n_gz) for step in range(n_gz)]
+    img_at = [wrapped(img + step, n_img) for step in range(n_img)]
+    above, below = gz_at[1 % n_gz], gz_at[-1]
 
     loads = [
         pltpu.make_async_copy(order_in, obuf.at[:, 1 : planes + 1], load_sem.at[0]),
         pltpu.make_async_copy(shift_in, sbuf.at[:, :, 1 : planes + 1], load_sem.at[1]),
     ]
-    for load in loads:
-        load.start()
+    loads[0].start()
 
     barrier = pltpu.get_barrier_semaphore()
 
@@ -104,11 +109,10 @@
         pl.semaphore_signal(
             barrier,
             inc=1,
-            device_id={"gz": lax.rem(gz + step, n_gz)},
+            device_id={"gz": gz_at[step]},
             device_id_type=MESH,
         )
     signal_near(barrier)
-    pl.semaphore_wait(barrier, n_gz - 1 + n_near)
 
     def spread(first, stop):
         for stage in range(first, stop):
@@ -135,9 +139,6 @@
     flat_down = halo(4, shift_in.at[0:2, :, 0], sbuf.at[0:2, :, top], below)
     first_halos = (order_down, order_up, lift_down)
     later_halos = (shift_up, flat_down)
-    for copy in first_halos:
-        copy.start()
-    spread(0, 1)
 
     misfit = misfit_ref[0]
     drive = latent_enthalpy * (kelvin_ref[0] - dissolution_limit_kelvin) / dissolution_limit_kelvin
@@ -149,12 +150,16 @@
         return sbuf[c, l, z].astype(jnp.float32)
 
     loads[0].wait()
+    loads[1].start()
     for l in range(images):
 
         def add_h(z, total, l=l):
             return total + lane_row(switching(order_at(l, z + 1)))
 
         hbuf[gz, l : l + 1] = lax.fori_loop(0, planes, add_h, jnp.zeros((1, LANES), jnp.float32))
+
+    pl.semaphore_wait(barrier, n_gz - 1 + n_near)
+    spread(0, 1)
 
     def h_copy(step):
         return pltpu.make_async_remote_copy(
@@ -162,12 +167,12 @@
             dst_ref=hbuf.at[gz],
             send_sem=h_send.at[step],
             recv_sem=h_recv.at[step],
-            device_id={"gz": lax.rem(gz + step, n_gz)},
+            device_id={"gz": gz_at[step]},
             device_id_type=MESH,
         )
 
     def h_arrival(step):
-        origin = lax.rem(gz + n_gz - step, n_gz)
+        origin = gz_at[n_gz - step]
         return pltpu.make_async_remote_copy(
             src_ref=hbuf.at[origin],
             dst_ref=hbuf.at[origin],
@@ -179,6 +184,8 @@
 
     for step in range(1, n_gz):
         h_copy(step).start()
+    for copy in first_halos:
+        copy.start()
     spread(1, 2)
 
     def move_plane(l, z):
@@ -242,7 +249,6 @@
         lax.fori_loop(0, images * 2, one, 0)
 
     loads[1].wait()
-    spread(2, 3)
 
     for step in range(1, n_gz):
         h_arrival(step).wait_recv()
@@ -259,7 +265,6 @@
             return carry
 
         lax.fori_loop(1, last, relax_inner, 0)
-    spread(3, n_img)
 
     def image_copy(slot, span, forward):
         return pltpu.make_async_remote_copy(
@@ -275,18 +280,23 @@
     forward_copies = [image_copy(i, span, True) for i, span in enumerate(spans)]
     backward_copies = [image_copy(3 + i, span, False) for i, span in enumerate(spans)]
 
-    def send_images(picks):
+    def send_back(i):
         @pl.when(has_previous)
         def _():
-            for i in picks:
-                backward_copies[i].start()
-
+            backward_copies[i].start()
+
+    def send_on(i):
         @pl.when(has_next)
         def _():
-            for i in picks:
-                forward_copies[i].start()
+            forward_copies[i].start()
+
+    def send_images(picks):
+        for i in picks:
+            send_back(i)
+            send_on(i)
 
     send_images((0,))
+    spread(2, 3)
 
     @pl.when(jnp.logical_not(has_previous))
     def _():
@@ -299,16 +309,21 @@
     inner_planes(move_plane)
 
     order_up.wait_recv()
-    for l in range(images):
+    for copy in later_halos:
+        copy.start()
+    relax(0, 0)
+    send_back(1)
+    for l in range(1, images):
         relax(l, 0)
-    send_images((1,))
+    send_on(1)
     order_down.wait_recv()
     lift_down.wait_recv()
-    for copy in later_halos:
-        copy.start()
-    for l in range(images):
+    relax(0, last)
+    send_back(2)
+    for l in range(1, images):
         relax(l, last)
-    send_images((2,))
+    send_on(2)
+    spread(3, n_img)
 
     def squares(l, first, stop, total):
         def add(z, total):
@@ -333,35 +348,38 @@
     total = squares(images - 1, 0, 1, total)
     gbuf[me, images - 1 : images] = squares(images - 1, last, planes, total)
 
-    def place(index):
-        return {"img": index // n_gz, "gz": lax.rem(index, n_gz)}
-
-    def g_copy(step):
+    def g_copy(to_img, to_gz):
         return pltpu.make_async_remote_copy(
             src_ref=gbuf.at[me],
             dst_ref=gbuf.at[me],
-            send_sem=g_send.at[step],
-            recv_sem=g_recv.at[step],
-            device_id=place(lax.rem(me + step, n_all)),
+            send_sem=g_send.at[0],
+            recv_sem=g_recv.at[0],
+            device_id={"img": to_img, "gz": to_gz},
             device_id_type=MESH,
         )
 
-    def g_arrival(step):
-        origin = lax.rem(me + n_all - step, n_all)
-        return pltpu.make_async_remote_copy(
-            src_ref=gbuf.at[origin],
-            dst_ref=gbuf.at[origin],
-            send_sem=g_send.at[step],
-            recv_sem=g_recv.at[step],
-            device_id=place(origin),
-            device_id_type=MESH,
-        )
-
-    def g_start(step, carry):
-        g_copy(step).start()
-        return carry
-
-    lax.fori_loop(1, n_all, g_start, 0, unroll=n_all <= 32)
+    if n_all <= 32:
+        for far in range(n_img - 1, -1, -1):
+            for near in range(n_gz - 1, -1, -1):
+                if far + near > 0:
+                    g_copy(img_at[far], gz_at[near]).start()
+    else:
+
+        def g_start(step, carry):
+            other = lax.rem(me + step, n_all)
+            g_copy(lax.div(other, n_gz), lax.rem(other, n_gz)).start()
+            return carry
+
+        lax.fori_loop(1, n_all, g_start, 0)
+
+    g_rows = pltpu.make_async_remote_copy(
+        src_ref=gbuf.at[0 : n_all - 1],
+        dst_ref=gbuf.at[0 : n_all - 1],
+        send_sem=g_send.at[0],
+        recv_sem=g_recv.at[0],
+        device_id={"gz": above},
+        device_id_type=MESH,
+    )
 
     for copy in later_halos:
         copy.wait_recv()
@@ -372,11 +390,7 @@
         for copy in forward_copies:
             copy.wait_recv()
 
-    def g_wait(step, carry):
-        g_arrival(step).wait_recv()
-        return carry
-
-    lax.fori_loop(1, n_all, g_wait, 0, unroll=n_all <= 32)
+    g_rows.wait_recv()
 
     total_images = images * n_img
     gaps = []
@@ -420,11 +434,7 @@
         for copy in forward_copies:
             copy.wait_send()
 
-    def g_done(step, carry):
-        g_copy(step).wait_send()
-        return carry
-
-    lax.fori_loop(1, n_all, g_done, 0, unroll=n_all <= 32)
+    g_rows.wait_send()
 
 
 def finish(relaxed_ref, moved_ref, weight_ref, string_out, moved_out, string_buf, sem):
@@ -484,8 +494,8 @@
             dma((6,)),
             dma((n_gz,)),
             dma((n_gz,)),
-            dma((n_img * n_gz,)),
-            dma((n_img * n_gz,)),
+            dma((1,)),
+            dma((1,)),
         ],
         compiler_params=pltpu.CompilerParams(
             collective_id=0, has_side_effects=True, vmem_limit_bytes=24 * 1024 * 1024

time: 22 us -> 20 us (0.909)
  Pallas kernels: 20 us -> 17.9 us
    pallas_call x1, Pallas kernels: 19 us -> 16.9 us  [shards(): pl.pallas_call(functools.partial(kernel, n_img, n_gz), out_shape=(jax.Sha...]
where the time goes in v3:
time: 20 us; the launch traced here: 19.8 us
  Pallas kernels  17.9 us (89%)
  between operations  1.93 us (10%)
    pallas_call x1, Pallas kernels, shards(): pl.pallas_call(functools.partial(kernel, n_img, n_gz), out_shape=(jax.Sha...  16.9 us
    pallas_call x1, Pallas kernels, shards(): pl.pallas_call(finish, out_shape=(jax.ShapeDtypeStruct(ordering_variable....  0.99 us

profile of v3, /device:TPU:0, one launch (start us, length us, event | category | flops | bytes accessed | tf_op | source)
XLA Modules:
  0.0 19.8 jit_solution(5639367234708774142)
XLA Ops:
  1.9 16.9 %shard_map.59 = (bf16[4,4,64,256]{3,2,1,0:T(8,128)(2,1)S(1)}, bf16[3,2,4,64,256]{4,3,2,1,0:T(8,128)(2,1)S(1)}, f32[4,256]{1,0:T(4,128)S(1)}) custom-call(f32[1]{0:T(128)S(6)} %copy.6.misfit_ref, f32[1]{0:T(128)S(6)} %copy.7.kelvin_ref, bf16[2,4,64,256]{3,2,1,0:T(8,128)(2,1)} %order_in.1, bf16[3,2,4,64,256]{4,3,2,1,0:T(8,128)(2,1)} %shift_in.1), custom_call_target="tpu_custom_call" | custom-call | tf_op jit(solution)/shard_map/pallas_call | solution.py:470
  18.8 1.0 %shard_map.60 = (bf16[2,4,64,256]{3,2,1,0:T(8,128)(2,1)}, bf16[3,2,4,64,256]{4,3,2,1,0:T(8,128)(2,1)}) custom-call(bf16[4,4,64,256]{3,2,1,0:T(8,128)(2,1)S(1)} %get-tuple-element.5.relaxed_ref, bf16[3,2,4,64,256]{4,3,2,1,0:T(8,128)(2,1)S(1)} %get-tuple-element.6.moved_ref, f32[4,256]{1,0:T(4,128)S(1)} %get-tuple-element.7.weight_ref), custom_call_target="tpu_custom_call" | custom-call | tf_op jit(solution)/shard_map/pallas_call | solution.py:504
